TPU v7x, 256 devices: a whole 4x4x8 slice. The times are simulated.
256 devices in a mesh: frow: 8 (over z_lo, core), fcol: 32 (over x, z_hi, y).
Axes of the slice: x: 4, y: 4, z: 8 (z_hi: 2, z_lo: 4; z = z_hi * 4 + z_lo), core: 2. Of those that a mesh axis runs over, the one named last changes fastest.
Arguments:
- right_side: float32 [64, 1024, 256], P('frow', 'fcol'), may hold values from -6 to 6
- noise_weight: float32 [64, 1024, 256], P('frow', 'fcol'), may hold values from 3 to 4.5
- stencils: bfloat16 [9, 256, 256], replicated, may hold values from -1 to 1, as said below
- neighbours: int32 [64, 1024, 9], P('frow', 'fcol'), may hold values from -1 to 65535, as said below
Outputs:
- solution: float32 [64, 1024, 256], P('frow', 'fcol')
- coarse_residual: float32 [32, 512, 256], P('frow')
Inputs may be any that keep to these rules, and one draw needn't show every extreme that they name: `neighbours`: each entry is -1 (an empty slot) or the index r * 1024 + c of the tile at row r = own row + k // 3 - 1 and column c = own column + k % 3 - 1 for slot k; slot 4 always holds the tile itself; if tile t holds tile s in slot k, then s holds t in slot 8 - k. stencils[8 - k] is the transpose of stencils[k], and stencils[4] is symmetric.
All inputs are finite; a program needn't handle non-finite values.
Results may differ from a plain program's by a relative error of at most 0.0031.
Values may be sent and summed in bfloat16 or wider, within the bound.
A program may use at most 64 MiB of HBM per device.

v0:
```python
import jax
import jax.numpy as jnp
from jax import lax
from jax.sharding import PartitionSpec as P

DEG = 3
lower_edge = 1.5
upper_edge = 6.0


def with_halo(cells, sides, width):
    for axis, dim in sides:
        count = lax.axis_size(axis)
        ends = count - 1
        head = lax.slice_in_dim(cells, 0, width, axis=dim)
        tail = lax.slice_in_dim(cells, cells.shape[dim] - width, cells.shape[dim], axis=dim)
        cells = jnp.concatenate(
            [
                lax.ppermute(tail, axis, [(i, (i + 1) % count) for i in range(ends)]),
                cells,
                lax.ppermute(head, axis, [((i + 1) % count, i) for i in range(ends)]),
            ],
            axis=dim,
        )
    return cells


def restrict(paired_block):
    height, width, doubled = paired_block.shape
    pixels = doubled // 2
    summed = jnp.sum(paired_block.reshape(height // 2, 2, width, 2, pixels // 4, 4), axis=5)
    return jnp.transpose(summed, (0, 2, 1, 3, 4)).reshape(height // 2, width, pixels)


def smooth(right_side, operate):
    center = 0.5 * (upper_edge + lower_edge)
    half_width = 0.5 * (upper_edge - lower_edge)
    spread_ratio = center / half_width
    solution = jnp.zeros_like(right_side)
    residual = right_side
    for sweep_index in range(2):
        ratio_now = 1.0 / spread_ratio
        direction = residual / center
        for step_index in range(DEG):
            solution = solution + direction
            residual = residual - operate(direction)
            if step_index < DEG - 1:
                ratio_next = 1.0 / (2.0 * spread_ratio - ratio_now)
                direction = (
                    ratio_next * ratio_now * direction + 2.0 * ratio_next / half_width * residual
                )
                ratio_now = ratio_next
    return (solution, residual)


def body(right_side, noise_weight, stencils, neighbours):
    tile_rows, tile_cols, pixels = right_side.shape
    slots = stencils.shape[0]
    grid_cols = tile_cols * lax.axis_size("fcol")
    row_anchor = lax.axis_index("frow") * tile_rows
    col_anchor = lax.axis_index("fcol") * tile_cols
    padded_count = (tile_rows + 2) * (tile_cols + 2)
    local_row = neighbours // grid_cols - row_anchor + 1
    local_col = neighbours % grid_cols - col_anchor + 1
    targets = jnp.where(
        neighbours < 0, padded_count, local_row * (tile_cols + 2) + local_col
    ).reshape(-1)
    stencil_matrix = stencils.reshape(slots * pixels, pixels)

    def operate(direction):
        rounded = direction.astype(jnp.bfloat16)
        padded = with_halo(rounded, (("frow", 0), ("fcol", 1)), 1)
        flattened = jnp.concatenate(
            [padded.reshape(padded_count, pixels), jnp.zeros((1, pixels), jnp.bfloat16)], 0
        )
        picked = jnp.take(flattened, targets, axis=0).reshape(tile_rows * tile_cols, slots * pixels)
        coupled = jnp.dot(picked, stencil_matrix, preferred_element_type=jnp.float32)
        return noise_weight * direction + coupled.reshape(tile_rows, tile_cols, pixels)

    solution, residual = smooth(right_side, operate)
    paired = residual.reshape(tile_rows, tile_cols // 2, 2 * pixels)
    coarse_residual = lax.all_gather(restrict(paired), "fcol", axis=1, tiled=True)
    return (solution, coarse_residual)


def solution(mesh):
    placed = (P("frow", "fcol", None), P("frow", "fcol", None), P(), P("frow", "fcol", None))
    return jax.shard_map(
        body,
        mesh=mesh,
        in_specs=placed,
        out_specs=(P("frow", "fcol", None), P("frow", None, None)),
        check_vma=False,
    )
```

profile of v0, /device:TPU:2, one launch (start us, length us, event | category | flops | bytes accessed | tf_op | source)
XLA Modules:
  0.0 339.4 jit_solution(16433742648850729699)
XLA Ops:
  12.5 2.3 collective-permute-done.1
  14.9 3.5 %collective-permute-start.2 = (bf16[10,1,256]{2,1,0:T(2,128)(2,1)S(1)}, bf16[10,1,256]{2,1,0:T(2,128)(2,1)S(1)}, u32[]{:S(2)}, u32[]{:S(2)}) collective-permute-start(bf16[10,1,256]{2,1,0:T(2,128)(2,1)S(1)} %get-tuple-element.15), channel_id=1, source_target_pairs={{0,1},{1,2},{2,3},{3,4},{4,5},{5,6},{6,7},{7,8},{8,9},{9,10},{10,1... | collective-permute-start | bytes 15368 | tf_op jit(solution)/shard_map/ppermute | solution.py:19
  18.3 9.3 %collective-permute-start.3 = (bf16[10,1,256]{2,1,0:T(2,128)(2,1)S(1)}, bf16[10,1,256]{2,1,0:T(2,128)(2,1)S(1)}, u32[]{:S(2)}, u32[]{:S(2)}) collective-permute-start(bf16[10,1,256]{2,1,0:T(2,128)(2,1)S(1)} %get-tuple-element.16), channel_id=1, source_target_pairs={{1,0},{2,1},{3,2},{4,3},{5,4},{6,5},{7,6},{8,7},{9,8},{10,9},{11,1... | collective-permute-start | bytes 15368 | tf_op jit(solution)/shard_map/ppermute | solution.py:21
  29.2 6.9 %gather_fusion = bf16[2304,256]{1,0:T(8,128)(2,1)S(1)} fusion(bf16[341,256]{1,0:T(8,128)(2,1)S(1)} %concatenate.56, s32[3072]{0:T(1024)S(1)} %pad_clamp_fusion), kind=kCustom, calls=%fused_computation.clone | custom fusion | bytes 2368512 | tf_op jit(solution)/shard_map/jit(_take)/gather | solution.py:76
  38.1 2.7 dot_general.30
  41.3 3.3 collective-permute-start.4
  46.0 2.4 collective-permute-done.5
  50.3 11.1 %collective-permute-start.7 = (bf16[10,1,256]{2,1,0:T(2,128)(2,1)S(1)}, bf16[10,1,256]{2,1,0:T(2,128)(2,1)S(1)}, u32[]{:S(2)}, u32[]{:S(2)}) collective-permute-start(bf16[10,1,256]{2,1,0:T(2,128)(2,1)S(1)} %get-tuple-element.14), channel_id=1, source_target_pairs={{1,0},{2,1},{3,2},{4,3},{5,4},{6,5},{7,6},{8,7},{9,8},{10,9},{11,1... | collective-permute-start | bytes 15368 | tf_op jit(solution)/shard_map/ppermute | solution.py:21
  63.0 6.9 %gather_fusion.1 = bf16[2304,256]{1,0:T(8,128)(2,1)S(1)} fusion(bf16[341,256]{1,0:T(8,128)(2,1)S(1)} %concatenate.59, s32[3072]{0:T(1024)S(1)} %pad_clamp_fusion), kind=kCustom, calls=%fused_computation.1.clone | custom fusion | bytes 2368512 | tf_op jit(solution)/shard_map/jit(_take)/gather | solution.py:76
  71.9 2.7 dot_general.32
  75.8 3.5 %collective-permute-start.8 = (bf16[1,32,256]{2,1,0:T(8,128)(2,1)S(1)}, bf16[1,32,256]{2,1,0:T(8,128)(2,1)S(1)}, u32[]{:S(2)}, u32[]{:S(2)}) collective-permute-start(bf16[1,32,256]{2,1,0:T(8,128)(2,1)S(1)} %get-tuple-element.23), channel_id=1, source_target_pairs={{0,32},{32,64},{64,96},{96,128},{128,160},{160,192},{192,224},{1,3... | collective-permute-start | bytes 49160 | tf_op jit(solution)/shard_map/ppermute | solution.py:19
  82.8 2.7 collective-permute-start.10
  85.5 10.3 %collective-permute-start.11 = (bf16[10,1,256]{2,1,0:T(2,128)(2,1)S(1)}, bf16[10,1,256]{2,1,0:T(2,128)(2,1)S(1)}, u32[]{:S(2)}, u32[]{:S(2)}) collective-permute-start(bf16[10,1,256]{2,1,0:T(2,128)(2,1)S(1)} %get-tuple-element.12), channel_id=1, source_target_pairs={{1,0},{2,1},{3,2},{4,3},{5,4},{6,5},{7,6},{8,7},{9,8},{10,9},{11,1... | collective-permute-start | bytes 15368 | tf_op jit(solution)/shard_map/ppermute | solution.py:21
  97.4 7.5 %gather_fusion.2 = bf16[2304,256]{1,0:T(8,128)(2,1)} fusion(bf16[341,256]{1,0:T(8,128)(2,1)S(1)} %concatenate.62, s32[3072]{0:T(1024)S(1)} %pad_clamp_fusion), kind=kCustom, calls=%fused_computation.2.clone | custom fusion | bytes 2368512 | tf_op jit(solution)/shard_map/jit(_take)/gather | solution.py:76
  104.8 2.3 broadcast_select_fusion.3
  111.1 3.5 %collective-permute-start.12 = (bf16[1,32,256]{2,1,0:T(8,128)(2,1)S(1)}, bf16[1,32,256]{2,1,0:T(8,128)(2,1)S(1)}, u32[]{:S(2)}, u32[]{:S(2)}) collective-permute-start(bf16[1,32,256]{2,1,0:T(8,128)(2,1)S(1)} %get-tuple-element.21), channel_id=1, source_target_pairs={{0,32},{32,64},{64,96},{96,128},{128,160},{160,192},{192,224},{1,3... | collective-permute-start | bytes 49160 | tf_op jit(solution)/shard_map/ppermute | solution.py:19
  120.0 11.3 %collective-permute-start.15 = (bf16[10,1,256]{2,1,0:T(2,128)(2,1)S(1)}, bf16[10,1,256]{2,1,0:T(2,128)(2,1)S(1)}, u32[]{:S(2)}, u32[]{:S(2)}) collective-permute-start(bf16[10,1,256]{2,1,0:T(2,128)(2,1)S(1)} %get-tuple-element.10), channel_id=1, source_target_pairs={{1,0},{2,1},{3,2},{4,3},{5,4},{6,5},{7,6},{8,7},{9,8},{10,9},{11,1... | collective-permute-start | bytes 15368 | tf_op jit(solution)/shard_map/ppermute | solution.py:21
  132.7 6.9 %gather_fusion.3 = bf16[2304,256]{1,0:T(8,128)(2,1)S(1)} fusion(bf16[341,256]{1,0:T(8,128)(2,1)S(1)} %concatenate.65, s32[3072]{0:T(1024)S(1)} %pad_clamp_fusion), kind=kCustom, calls=%fused_computation.3.clone | custom fusion | bytes 2368512 | tf_op jit(solution)/shard_map/jit(_take)/gather | solution.py:76
  141.6 2.7 dot_general.36
  145.5 3.5 %collective-permute-start.16 = (bf16[1,32,256]{2,1,0:T(8,128)(2,1)S(1)}, bf16[1,32,256]{2,1,0:T(8,128)(2,1)S(1)}, u32[]{:S(2)}, u32[]{:S(2)}) collective-permute-start(bf16[1,32,256]{2,1,0:T(8,128)(2,1)S(1)} %get-tuple-element.19), channel_id=1, source_target_pairs={{0,32},{32,64},{64,96},{96,128},{128,160},{160,192},{192,224},{1,3... | collective-permute-start | bytes 49160 | tf_op jit(solution)/shard_map/ppermute | solution.py:19
  154.4 11.1 %collective-permute-start.19 = (bf16[10,1,256]{2,1,0:T(2,128)(2,1)S(1)}, bf16[10,1,256]{2,1,0:T(2,128)(2,1)S(1)}, u32[]{:S(2)}, u32[]{:S(2)}) collective-permute-start(bf16[10,1,256]{2,1,0:T(2,128)(2,1)S(1)} %get-tuple-element.8), channel_id=1, source_target_pairs={{1,0},{2,1},{3,2},{4,3},{5,4},{6,5},{7,6},{8,7},{9,8},{10,9},{11,1... | collective-permute-start | bytes 15368 | tf_op jit(solution)/shard_map/ppermute | solution.py:21
  167.0 6.9 %gather_fusion.4 = bf16[2304,256]{1,0:T(8,128)(2,1)S(1)} fusion(bf16[341,256]{1,0:T(8,128)(2,1)S(1)} %concatenate.68, s32[3072]{0:T(1024)S(1)} %pad_clamp_fusion), kind=kCustom, calls=%fused_computation.4.clone | custom fusion | bytes 2368512 | tf_op jit(solution)/shard_map/jit(_take)/gather | solution.py:76
  176.0 2.7 dot_general.38
  178.6 2.5 fusion.7
  181.1 3.5 %collective-permute-start.20 = (bf16[1,32,256]{2,1,0:T(8,128)(2,1)S(1)}, bf16[1,32,256]{2,1,0:T(8,128)(2,1)S(1)}, u32[]{:S(2)}, u32[]{:S(2)}) collective-permute-start(bf16[1,32,256]{2,1,0:T(8,128)(2,1)S(1)} %get-tuple-element.17), channel_id=1, source_target_pairs={{0,32},{32,64},{64,96},{96,128},{128,160},{160,192},{192,224},{1,3... | collective-permute-start | bytes 49160 | tf_op jit(solution)/shard_map/ppermute | solution.py:19
  190.0 11.3 %collective-permute-start.23 = (bf16[10,1,256]{2,1,0:T(2,128)(2,1)S(1)}, bf16[10,1,256]{2,1,0:T(2,128)(2,1)S(1)}, u32[]{:S(2)}, u32[]{:S(2)}) collective-permute-start(bf16[10,1,256]{2,1,0:T(2,128)(2,1)S(1)} %get-tuple-element.6), channel_id=1, source_target_pairs={{1,0},{2,1},{3,2},{4,3},{5,4},{6,5},{7,6},{8,7},{9,8},{10,9},{11,1... | collective-permute-start | bytes 15368 | tf_op jit(solution)/shard_map/ppermute | solution.py:21
  202.7 6.9 %gather_fusion.5 = bf16[2304,256]{1,0:T(8,128)(2,1)S(1)} fusion(bf16[341,256]{1,0:T(8,128)(2,1)S(1)} %concatenate.71, s32[3072]{0:T(1024)S(1)} %pad_clamp_fusion), kind=kCustom, calls=%fused_computation.5.clone | custom fusion | bytes 2368512 | tf_op jit(solution)/shard_map/jit(_take)/gather | solution.py:76
  211.6 2.7 dot_general.40
  216.5 10.9 %reshape_reshape.3 = f32[4,2,16,2,64,4]{5,4,3,2,1,0:T(8,128)} reshape(f32[8,32,256]{2,1,0:T(8,128)} %fusion) | data formatting | bytes 524288 | tf_op jit(solution)/shard_map/reshape;reshape | solution.py:31
  227.4 5.7 %reduce_sum.9 = f32[4,2,16,2,64]{4,3,2,1,0:T(2,128)S(1)} reduce(f32[4,2,16,2,64,4]{5,4,3,2,1,0:T(8,128)} %reshape_reshape.3, f32[]{:T(128)} %constant.74.clone.1), dimensions={5}, to_apply=%region_0.2 | reduce | flops 49152 | bytes 327684 | tf_op jit(solution)/shard_map/reduce_sum | solution.py:31
  233.9 95.6 %all-gather.2.cloned.1.call-done = f32[4,512,256]{2,1,0:T(8,128)} async-done(((f32[4,16,256]{2,1,0:T(8,128)}), f32[4,512,256]{2,1,0:T(8,128)}) %all-gather.2.cloned.1.call-update) | async-done | bytes 2097168 | tf_op jit(solution)/shard_map/all_gather | solution.py:82
  329.5 3.0 copy.11
  (95 shorter events, 56.9 us)
Async XLA Ops:
  7.2 33.6 %copy-start = (bf16[9,256,256]{2,1,0:T(8,128)(2,1)S(1)}, bf16[9,256,256]{2,1,0:T(8,128)(2,1)}, u32[]{:S(2)}) copy-start(bf16[9,256,256]{2,1,0:T(8,128)(2,1)} %param.8) | copy-start | bytes 3538948
  7.2 322.3 %all-gather.2.cloned.1.call-start = ((), (), s32[]{:S(2)}) async-start(), calls=%async_computation | async-start | bytes 2162688 | tf_op jit(solution)/shard_map/all_gather | solution.py:82
  8.3 4.2 %collective-permute-start = (bf16[1,32,256]{2,1,0:T(8,128)(2,1)S(1)}, bf16[1,32,256]{2,1,0:T(8,128)(2,1)S(1)}, u32[]{:S(2)}, u32[]{:S(2)}) collective-permute-start(bf16[1,32,256]{2,1,0:T(8,128)(2,1)S(1)} %get-tuple-element.27), channel_id=1, source_target_pairs={{0,32},{32,64},{64,96},{96,128},{128,160},{160,192},{192,224},{1,3... | collective-permute-start | bytes 49160 | tf_op jit(solution)/shard_map/ppermute | solution.py:19
  10.0 4.8 %collective-permute-start.1 = (bf16[1,32,256]{2,1,0:T(8,128)(2,1)S(1)}, bf16[1,32,256]{2,1,0:T(8,128)(2,1)S(1)}, u32[]{:S(2)}, u32[]{:S(2)}) collective-permute-start(bf16[1,32,256]{2,1,0:T(8,128)(2,1)S(1)} %get-tuple-element.28), channel_id=1, source_target_pairs={{32,0},{64,32},{96,64},{128,96},{160,128},{192,160},{224,192},{33,... | collective-permute-start | bytes 49160 | tf_op jit(solution)/shard_map/ppermute | solution.py:21
  14.9 12.8 %collective-permute-start.2 = (bf16[10,1,256]{2,1,0:T(2,128)(2,1)S(1)}, bf16[10,1,256]{2,1,0:T(2,128)(2,1)S(1)}, u32[]{:S(2)}, u32[]{:S(2)}) collective-permute-start(bf16[10,1,256]{2,1,0:T(2,128)(2,1)S(1)} %get-tuple-element.15), channel_id=1, source_target_pairs={{0,1},{1,2},{2,3},{3,4},{4,5},{5,6},{6,7},{7,8},{8,9},{9,10},{10,1... | collective-permute-start | bytes 15368 | tf_op jit(solution)/shard_map/ppermute | solution.py:19
  18.3 10.6 %collective-permute-start.3 = (bf16[10,1,256]{2,1,0:T(2,128)(2,1)S(1)}, bf16[10,1,256]{2,1,0:T(2,128)(2,1)S(1)}, u32[]{:S(2)}, u32[]{:S(2)}) collective-permute-start(bf16[10,1,256]{2,1,0:T(2,128)(2,1)S(1)} %get-tuple-element.16), channel_id=1, source_target_pairs={{1,0},{2,1},{3,2},{4,3},{5,4},{6,5},{7,6},{8,7},{9,8},{10,9},{11,1... | collective-permute-start | bytes 15368 | tf_op jit(solution)/shard_map/ppermute | solution.py:21
  38.1 2.7 copy-start.1
  38.1 2.7 copy-start.2
  41.3 33.2 %copy-start.3 = (f32[8,32,256]{2,1,0:T(8,128)}, f32[8,32,256]{2,1,0:T(8,128)S(1)}, u32[]{:S(2)}) copy-start(f32[8,32,256]{2,1,0:T(8,128)S(1)} %get-tuple-element.30) | copy-start | bytes 786436
  41.3 4.6 %collective-permute-start.4 = (bf16[1,32,256]{2,1,0:T(8,128)(2,1)S(1)}, bf16[1,32,256]{2,1,0:T(8,128)(2,1)S(1)}, u32[]{:S(2)}, u32[]{:S(2)}) collective-permute-start(bf16[1,32,256]{2,1,0:T(8,128)(2,1)S(1)} %get-tuple-element.25), channel_id=1, source_target_pairs={{0,32},{32,64},{64,96},{96,128},{128,160},{160,192},{192,224},{1,3... | collective-permute-start | bytes 49160 | tf_op jit(solution)/shard_map/ppermute | solution.py:19
  44.7 3.7 %collective-permute-start.5 = (bf16[1,32,256]{2,1,0:T(8,128)(2,1)S(1)}, bf16[1,32,256]{2,1,0:T(8,128)(2,1)S(1)}, u32[]{:S(2)}, u32[]{:S(2)}) collective-permute-start(bf16[1,32,256]{2,1,0:T(8,128)(2,1)S(1)} %get-tuple-element.26), channel_id=1, source_target_pairs={{32,0},{64,32},{96,64},{128,96},{160,128},{192,160},{224,192},{33,... | collective-permute-start | bytes 49160 | tf_op jit(solution)/shard_map/ppermute | solution.py:21
  48.4 13.1 %collective-permute-start.6 = (bf16[10,1,256]{2,1,0:T(2,128)(2,1)S(1)}, bf16[10,1,256]{2,1,0:T(2,128)(2,1)S(1)}, u32[]{:S(2)}, u32[]{:S(2)}) collective-permute-start(bf16[10,1,256]{2,1,0:T(2,128)(2,1)S(1)} %get-tuple-element.13), channel_id=1, source_target_pairs={{0,1},{1,2},{2,3},{3,4},{4,5},{5,6},{6,7},{7,8},{8,9},{9,10},{10,1... | collective-permute-start | bytes 15368 | tf_op jit(solution)/shard_map/ppermute | solution.py:19
  50.3 12.5 %collective-permute-start.7 = (bf16[10,1,256]{2,1,0:T(2,128)(2,1)S(1)}, bf16[10,1,256]{2,1,0:T(2,128)(2,1)S(1)}, u32[]{:S(2)}, u32[]{:S(2)}) collective-permute-start(bf16[10,1,256]{2,1,0:T(2,128)(2,1)S(1)} %get-tuple-element.14), channel_id=1, source_target_pairs={{1,0},{2,1},{3,2},{4,3},{5,4},{6,5},{7,6},{8,7},{9,8},{10,9},{11,1... | collective-permute-start | bytes 15368 | tf_op jit(solution)/shard_map/ppermute | solution.py:21
  75.8 4.8 %collective-permute-start.8 = (bf16[1,32,256]{2,1,0:T(8,128)(2,1)S(1)}, bf16[1,32,256]{2,1,0:T(8,128)(2,1)S(1)}, u32[]{:S(2)}, u32[]{:S(2)}) collective-permute-start(bf16[1,32,256]{2,1,0:T(8,128)(2,1)S(1)} %get-tuple-element.23), channel_id=1, source_target_pairs={{0,32},{32,64},{64,96},{96,128},{128,160},{160,192},{192,224},{1,3... | collective-permute-start | bytes 49160 | tf_op jit(solution)/shard_map/ppermute | solution.py:19
  79.3 3.5 %collective-permute-start.9 = (bf16[1,32,256]{2,1,0:T(8,128)(2,1)S(1)}, bf16[1,32,256]{2,1,0:T(8,128)(2,1)S(1)}, u32[]{:S(2)}, u32[]{:S(2)}) collective-permute-start(bf16[1,32,256]{2,1,0:T(8,128)(2,1)S(1)} %get-tuple-element.24), channel_id=1, source_target_pairs={{32,0},{64,32},{96,64},{128,96},{160,128},{192,160},{224,192},{33,... | collective-permute-start | bytes 49160 | tf_op jit(solution)/shard_map/ppermute | solution.py:21
  82.8 13.1 %collective-permute-start.10 = (bf16[10,1,256]{2,1,0:T(2,128)(2,1)S(1)}, bf16[10,1,256]{2,1,0:T(2,128)(2,1)S(1)}, u32[]{:S(2)}, u32[]{:S(2)}) collective-permute-start(bf16[10,1,256]{2,1,0:T(2,128)(2,1)S(1)} %get-tuple-element.11), channel_id=1, source_target_pairs={{0,1},{1,2},{2,3},{3,4},{4,5},{5,6},{6,7},{7,8},{8,9},{9,10},{10,1... | collective-permute-start | bytes 15368 | tf_op jit(solution)/shard_map/ppermute | solution.py:19
  85.5 11.7 %collective-permute-start.11 = (bf16[10,1,256]{2,1,0:T(2,128)(2,1)S(1)}, bf16[10,1,256]{2,1,0:T(2,128)(2,1)S(1)}, u32[]{:S(2)}, u32[]{:S(2)}) collective-permute-start(bf16[10,1,256]{2,1,0:T(2,128)(2,1)S(1)} %get-tuple-element.12), channel_id=1, source_target_pairs={{1,0},{2,1},{3,2},{4,3},{5,4},{6,5},{7,6},{8,7},{9,8},{10,9},{11,1... | collective-permute-start | bytes 15368 | tf_op jit(solution)/shard_map/ppermute | solution.py:21
  111.1 4.8 %collective-permute-start.12 = (bf16[1,32,256]{2,1,0:T(8,128)(2,1)S(1)}, bf16[1,32,256]{2,1,0:T(8,128)(2,1)S(1)}, u32[]{:S(2)}, u32[]{:S(2)}) collective-permute-start(bf16[1,32,256]{2,1,0:T(8,128)(2,1)S(1)} %get-tuple-element.21), channel_id=1, source_target_pairs={{0,32},{32,64},{64,96},{96,128},{128,160},{160,192},{192,224},{1,3... | collective-permute-start | bytes 49160 | tf_op jit(solution)/shard_map/ppermute | solution.py:19
  114.6 3.5 %collective-permute-start.13 = (bf16[1,32,256]{2,1,0:T(8,128)(2,1)S(1)}, bf16[1,32,256]{2,1,0:T(8,128)(2,1)S(1)}, u32[]{:S(2)}, u32[]{:S(2)}) collective-permute-start(bf16[1,32,256]{2,1,0:T(8,128)(2,1)S(1)} %get-tuple-element.22), channel_id=1, source_target_pairs={{32,0},{64,32},{96,64},{128,96},{160,128},{192,160},{224,192},{33,... | collective-permute-start | bytes 49160 | tf_op jit(solution)/shard_map/ppermute | solution.py:21
  118.1 13.2 %collective-permute-start.14 = (bf16[10,1,256]{2,1,0:T(2,128)(2,1)S(1)}, bf16[10,1,256]{2,1,0:T(2,128)(2,1)S(1)}, u32[]{:S(2)}, u32[]{:S(2)}) collective-permute-start(bf16[10,1,256]{2,1,0:T(2,128)(2,1)S(1)} %get-tuple-element.9), channel_id=1, source_target_pairs={{0,1},{1,2},{2,3},{3,4},{4,5},{5,6},{6,7},{7,8},{8,9},{9,10},{10,1... | collective-permute-start | bytes 15368 | tf_op jit(solution)/shard_map/ppermute | solution.py:19
  120.0 12.5 %collective-permute-start.15 = (bf16[10,1,256]{2,1,0:T(2,128)(2,1)S(1)}, bf16[10,1,256]{2,1,0:T(2,128)(2,1)S(1)}, u32[]{:S(2)}, u32[]{:S(2)}) collective-permute-start(bf16[10,1,256]{2,1,0:T(2,128)(2,1)S(1)} %get-tuple-element.10), channel_id=1, source_target_pairs={{1,0},{2,1},{3,2},{4,3},{5,4},{6,5},{7,6},{8,7},{9,8},{10,9},{11,1... | collective-permute-start | bytes 15368 | tf_op jit(solution)/shard_map/ppermute | solution.py:21
  145.5 4.8 %collective-permute-start.16 = (bf16[1,32,256]{2,1,0:T(8,128)(2,1)S(1)}, bf16[1,32,256]{2,1,0:T(8,128)(2,1)S(1)}, u32[]{:S(2)}, u32[]{:S(2)}) collective-permute-start(bf16[1,32,256]{2,1,0:T(8,128)(2,1)S(1)} %get-tuple-element.19), channel_id=1, source_target_pairs={{0,32},{32,64},{64,96},{96,128},{128,160},{160,192},{192,224},{1,3... | collective-permute-start | bytes 49160 | tf_op jit(solution)/shard_map/ppermute | solution.py:19
  149.0 3.5 %collective-permute-start.17 = (bf16[1,32,256]{2,1,0:T(8,128)(2,1)S(1)}, bf16[1,32,256]{2,1,0:T(8,128)(2,1)S(1)}, u32[]{:S(2)}, u32[]{:S(2)}) collective-permute-start(bf16[1,32,256]{2,1,0:T(8,128)(2,1)S(1)} %get-tuple-element.20), channel_id=1, source_target_pairs={{32,0},{64,32},{96,64},{128,96},{160,128},{192,160},{224,192},{33,... | collective-permute-start | bytes 49160 | tf_op jit(solution)/shard_map/ppermute | solution.py:21
  152.5 13.0 %collective-permute-start.18 = (bf16[10,1,256]{2,1,0:T(2,128)(2,1)S(1)}, bf16[10,1,256]{2,1,0:T(2,128)(2,1)S(1)}, u32[]{:S(2)}, u32[]{:S(2)}) collective-permute-start(bf16[10,1,256]{2,1,0:T(2,128)(2,1)S(1)} %get-tuple-element.7), channel_id=1, source_target_pairs={{0,1},{1,2},{2,3},{3,4},{4,5},{5,6},{6,7},{7,8},{8,9},{9,10},{10,1... | collective-permute-start | bytes 15368 | tf_op jit(solution)/shard_map/ppermute | solution.py:19
  154.4 12.5 %collective-permute-start.19 = (bf16[10,1,256]{2,1,0:T(2,128)(2,1)S(1)}, bf16[10,1,256]{2,1,0:T(2,128)(2,1)S(1)}, u32[]{:S(2)}, u32[]{:S(2)}) collective-permute-start(bf16[10,1,256]{2,1,0:T(2,128)(2,1)S(1)} %get-tuple-element.8), channel_id=1, source_target_pairs={{1,0},{2,1},{3,2},{4,3},{5,4},{6,5},{7,6},{8,7},{9,8},{10,9},{11,1... | collective-permute-start | bytes 15368 | tf_op jit(solution)/shard_map/ppermute | solution.py:21
  181.1 4.8 %collective-permute-start.20 = (bf16[1,32,256]{2,1,0:T(8,128)(2,1)S(1)}, bf16[1,32,256]{2,1,0:T(8,128)(2,1)S(1)}, u32[]{:S(2)}, u32[]{:S(2)}) collective-permute-start(bf16[1,32,256]{2,1,0:T(8,128)(2,1)S(1)} %get-tuple-element.17), channel_id=1, source_target_pairs={{0,32},{32,64},{64,96},{96,128},{128,160},{160,192},{192,224},{1,3... | collective-permute-start | bytes 49160 | tf_op jit(solution)/shard_map/ppermute | solution.py:19
  184.6 3.5 %collective-permute-start.21 = (bf16[1,32,256]{2,1,0:T(8,128)(2,1)S(1)}, bf16[1,32,256]{2,1,0:T(8,128)(2,1)S(1)}, u32[]{:S(2)}, u32[]{:S(2)}) collective-permute-start(bf16[1,32,256]{2,1,0:T(8,128)(2,1)S(1)} %get-tuple-element.18), channel_id=1, source_target_pairs={{32,0},{64,32},{96,64},{128,96},{160,128},{192,160},{224,192},{33,... | collective-permute-start | bytes 49160 | tf_op jit(solution)/shard_map/ppermute | solution.py:21
  188.1 13.3 %collective-permute-start.22 = (bf16[10,1,256]{2,1,0:T(2,128)(2,1)S(1)}, bf16[10,1,256]{2,1,0:T(2,128)(2,1)S(1)}, u32[]{:S(2)}, u32[]{:S(2)}) collective-permute-start(bf16[10,1,256]{2,1,0:T(2,128)(2,1)S(1)} %get-tuple-element.5), channel_id=1, source_target_pairs={{0,1},{1,2},{2,3},{3,4},{4,5},{5,6},{6,7},{7,8},{8,9},{9,10},{10,1... | collective-permute-start | bytes 15368 | tf_op jit(solution)/shard_map/ppermute | solution.py:19
  190.0 12.5 %collective-permute-start.23 = (bf16[10,1,256]{2,1,0:T(2,128)(2,1)S(1)}, bf16[10,1,256]{2,1,0:T(2,128)(2,1)S(1)}, u32[]{:S(2)}, u32[]{:S(2)}) collective-permute-start(bf16[10,1,256]{2,1,0:T(2,128)(2,1)S(1)} %get-tuple-element.6), channel_id=1, source_target_pairs={{1,0},{2,1},{3,2},{4,3},{5,4},{6,5},{7,6},{8,7},{9,8},{10,9},{11,1... | collective-permute-start | bytes 15368 | tf_op jit(solution)/shard_map/ppermute | solution.py:21
  211.6 2.7 copy-start.4
Sparse Core Ops, SparseCore 0:
  234.1 95.3 all-gather.1
where the time goes:
time: 341 us; the launch traced here: 339 us
  waiting for transfers between devices  117 us (34%)
  starting transfers between devices  105 us (31%)
  local copies, waits for them, and re-layouts  72.8 us (21%)
  other arithmetic  20.7 us (6%)
  between operations  14.7 us (4%)
  matrix products  9.38 us (3%)
    all_gather x1, waiting for transfers between devices, body(): lax.all_gather(restrict(paired), 'fcol', axis=1, tiled=True)  95.6 us
    ppermute x12, starting transfers between devices, with_halo(): lax.ppermute(head, axis, [((i + 1) % count, i) for i in range(ends)])  72.2 us
    gather x6, local copies, waits for them, and re-layouts, operate(): jnp.take(flattened, targets, axis=0)  41.8 us
    ppermute x12, starting transfers between devices, with_halo(): lax.ppermute(tail, axis, [(i, (i + 1) % count) for i in range(ends)])  33 us
    ppermute x12, waiting for transfers between devices, with_halo(): lax.ppermute(head, axis, [((i + 1) % count, i) for i in range(ends)])  21 us
    dot_general x6, local copies, waits for them, and re-layouts, operate(): jnp.dot(picked, stencil_matrix, preferred_element_type=jnp.float32)  15.5 us
    select_n x7, other arithmetic, operate(): jnp.take(flattened, targets, axis=0)  12.6 us
    another operation x1, local copies, waits for them, and re-layouts, restrict(): paired_block.reshape(height // 2, 2, width, 2, pixels // 4, 4)  10.9 us
  transfers between devices with their start and end apart: 25, of which 13 were waited for; matrix products, arithmetic and copies ran while one was open for 0% of the time, Pallas kernels for 0%

commit v1 on v0

--- a/solution.py
+++ b/solution.py
@@ -79,7 +79,9 @@
 
     solution, residual = smooth(right_side, operate)
     paired = residual.reshape(tile_rows, tile_cols // 2, 2 * pixels)
-    coarse_residual = lax.all_gather(restrict(paired), "fcol", axis=1, tiled=True)
+    coarse_residual = jnp.concatenate(
+        lax.all_to_all(jnp.stack([restrict(paired)] * lax.axis_size("fcol")), "fcol", 0, 0), axis=1
+    )
     return (solution, coarse_residual)
 
 

time: 341 us -> 298 us (0.87)
  the two profiles are of different devices: /device:TPU:2 before, /device:TPU:65 now
where the time goes in v1:
time: 298 us; the launch traced here: 296 us
  starting transfers between devices  77.8 us (26%)
  blocking collectives  76.7 us (26%)
  local copies, waits for them, and re-layouts  70.9 us (24%)
  waiting for transfers between devices  39.4 us (13%)
  other arithmetic  20.7 us (7%)
  matrix products  9.37 us (3%)
    all_to_all x1, blocking collectives, body(): lax.all_to_all(jnp.stack([restrict(paired)] * lax.axis_size('fcol')), 'fc...  76.7 us
    ppermute x12, starting transfers between devices, with_halo(): lax.ppermute(tail, axis, [(i, (i + 1) % count) for i in range(ends)])  58.2 us
    gather x6, local copies, waits for them, and re-layouts, operate(): jnp.take(flattened, targets, axis=0)  41.8 us
    ppermute x12, waiting for transfers between devices, with_halo(): lax.ppermute(head, axis, [((i + 1) % count, i) for i in range(ends)])  39.4 us
    ppermute x12, starting transfers between devices, with_halo(): lax.ppermute(head, axis, [((i + 1) % count, i) for i in range(ends)])  19.7 us
    dot_general x6, local copies, waits for them, and re-layouts, operate(): jnp.dot(picked, stencil_matrix, preferred_element_type=jnp.float32)  15.5 us
    select_n x7, other arithmetic, operate(): jnp.take(flattened, targets, axis=0)  12.6 us
    another operation x1, local copies, waits for them, and re-layouts, restrict(): paired_block.reshape(height // 2, 2, width, 2, pixels // 4, 4)  10.9 us
  transfers between devices with their start and end apart: 24, of which 12 were waited for; matrix products, arithmetic and copies ran while one was open for 0% of the time, Pallas kernels for 0%

profile of v1, /device:TPU:65, one launch (start us, length us, event | category | flops | bytes accessed | tf_op | source)
XLA Modules:
  0.0 296.2 jit_solution(4314874630144102110)
XLA Ops:
  1.7 4.1 %collective-permute-start = (bf16[1,32,256]{2,1,0:T(8,128)(2,1)S(1)}, bf16[1,32,256]{2,1,0:T(8,128)(2,1)S(1)}, u32[]{:S(2)}, u32[]{:S(2)}) collective-permute-start(bf16[1,32,256]{2,1,0:T(8,128)(2,1)S(1)} %get-tuple-element.27), channel_id=1, source_target_pairs={{0,32},{32,64},{64,96},{96,128},{128,160},{160,192},{192,224},{1,3... | collective-permute-start | bytes 49160 | tf_op jit(solution)/shard_map/ppermute | solution.py:19
  10.9 3.2 %collective-permute-start.2 = (bf16[10,1,256]{2,1,0:T(2,128)(2,1)S(1)}, bf16[10,1,256]{2,1,0:T(2,128)(2,1)S(1)}, u32[]{:S(2)}, u32[]{:S(2)}) collective-permute-start(bf16[10,1,256]{2,1,0:T(2,128)(2,1)S(1)} %get-tuple-element.15), channel_id=1, source_target_pairs={{0,1},{1,2},{2,3},{3,4},{4,5},{5,6},{6,7},{7,8},{8,9},{9,10},{10,1... | collective-permute-start | bytes 15368 | tf_op jit(solution)/shard_map/ppermute | solution.py:19
  15.5 3.1 %collective-permute-done.3 = bf16[10,1,256]{2,1,0:T(2,128)(2,1)S(1)} collective-permute-done((bf16[10,1,256]{2,1,0:T(2,128)(2,1)S(1)}, bf16[10,1,256]{2,1,0:T(2,128)(2,1)S(1)}, u32[]{:S(2)}, u32[]{:S(2)}) %collective-permute-start.3) | collective-permute-done | bytes 5152 | tf_op jit(solution)/shard_map/ppermute | solution.py:21
  18.7 6.9 %gather_fusion = bf16[2304,256]{1,0:T(8,128)(2,1)S(1)} fusion(bf16[341,256]{1,0:T(8,128)(2,1)S(1)} %concatenate.56, s32[3072]{0:T(1024)S(1)} %pad_clamp_fusion), kind=kCustom, calls=%fused_computation.clone | custom fusion | bytes 2368512 | tf_op jit(solution)/shard_map/jit(_take)/gather | solution.py:76
  30.9 3.4 %collective-permute-start.4 = (bf16[1,32,256]{2,1,0:T(8,128)(2,1)S(1)}, bf16[1,32,256]{2,1,0:T(8,128)(2,1)S(1)}, u32[]{:S(2)}, u32[]{:S(2)}) collective-permute-start(bf16[1,32,256]{2,1,0:T(8,128)(2,1)S(1)} %get-tuple-element.25), channel_id=1, source_target_pairs={{0,32},{32,64},{64,96},{96,128},{128,160},{160,192},{192,224},{1,3... | collective-permute-start | bytes 49160 | tf_op jit(solution)/shard_map/ppermute | solution.py:19
  36.2 3.1 %collective-permute-done.5 = bf16[1,32,256]{2,1,0:T(8,128)(2,1)S(1)} collective-permute-done((bf16[1,32,256]{2,1,0:T(8,128)(2,1)S(1)}, bf16[1,32,256]{2,1,0:T(8,128)(2,1)S(1)}, u32[]{:S(2)}, u32[]{:S(2)}) %collective-permute-start.5) | collective-permute-done | bytes 16416 | tf_op jit(solution)/shard_map/ppermute | solution.py:21
  39.4 3.2 %collective-permute-start.6 = (bf16[10,1,256]{2,1,0:T(2,128)(2,1)S(1)}, bf16[10,1,256]{2,1,0:T(2,128)(2,1)S(1)}, u32[]{:S(2)}, u32[]{:S(2)}) collective-permute-start(bf16[10,1,256]{2,1,0:T(2,128)(2,1)S(1)} %get-tuple-element.13), channel_id=1, source_target_pairs={{0,1},{1,2},{2,3},{3,4},{4,5},{5,6},{6,7},{7,8},{8,9},{9,10},{10,1... | collective-permute-start | bytes 15368 | tf_op jit(solution)/shard_map/ppermute | solution.py:19
  43.9 5.0 %collective-permute-done.7 = bf16[10,1,256]{2,1,0:T(2,128)(2,1)S(1)} collective-permute-done((bf16[10,1,256]{2,1,0:T(2,128)(2,1)S(1)}, bf16[10,1,256]{2,1,0:T(2,128)(2,1)S(1)}, u32[]{:S(2)}, u32[]{:S(2)}) %collective-permute-start.7) | collective-permute-done | bytes 5152 | tf_op jit(solution)/shard_map/ppermute | solution.py:21
  49.0 6.9 %gather_fusion.1 = bf16[2304,256]{1,0:T(8,128)(2,1)S(1)} fusion(bf16[341,256]{1,0:T(8,128)(2,1)S(1)} %concatenate.59, s32[3072]{0:T(1024)S(1)} %pad_clamp_fusion), kind=kCustom, calls=%fused_computation.1.clone | custom fusion | bytes 2368512 | tf_op jit(solution)/shard_map/jit(_take)/gather | solution.py:76
  61.8 2.9 collective-permute-start.8
  66.7 3.1 %collective-permute-done.9 = bf16[1,32,256]{2,1,0:T(8,128)(2,1)S(1)} collective-permute-done((bf16[1,32,256]{2,1,0:T(8,128)(2,1)S(1)}, bf16[1,32,256]{2,1,0:T(8,128)(2,1)S(1)}, u32[]{:S(2)}, u32[]{:S(2)}) %collective-permute-start.9) | collective-permute-done | bytes 16416 | tf_op jit(solution)/shard_map/ppermute | solution.py:21
  69.8 9.7 %collective-permute-start.10 = (bf16[10,1,256]{2,1,0:T(2,128)(2,1)S(1)}, bf16[10,1,256]{2,1,0:T(2,128)(2,1)S(1)}, u32[]{:S(2)}, u32[]{:S(2)}) collective-permute-start(bf16[10,1,256]{2,1,0:T(2,128)(2,1)S(1)} %get-tuple-element.11), channel_id=1, source_target_pairs={{0,1},{1,2},{2,3},{3,4},{4,5},{5,6},{6,7},{7,8},{8,9},{9,10},{10,1... | collective-permute-start | bytes 15368 | tf_op jit(solution)/shard_map/ppermute | solution.py:19
  80.8 3.6 %collective-permute-done.11 = bf16[10,1,256]{2,1,0:T(2,128)(2,1)S(1)} collective-permute-done((bf16[10,1,256]{2,1,0:T(2,128)(2,1)S(1)}, bf16[10,1,256]{2,1,0:T(2,128)(2,1)S(1)}, u32[]{:S(2)}, u32[]{:S(2)}) %collective-permute-start.11) | collective-permute-done | bytes 5152 | tf_op jit(solution)/shard_map/ppermute | solution.py:21
  84.5 7.5 %gather_fusion.2 = bf16[2304,256]{1,0:T(8,128)(2,1)} fusion(bf16[341,256]{1,0:T(8,128)(2,1)S(1)} %concatenate.62, s32[3072]{0:T(1024)S(1)} %pad_clamp_fusion), kind=kCustom, calls=%fused_computation.2.clone | custom fusion | bytes 2368512 | tf_op jit(solution)/shard_map/jit(_take)/gather | solution.py:76
  98.2 2.9 collective-permute-start.12
  103.1 3.1 %collective-permute-done.13 = bf16[1,32,256]{2,1,0:T(8,128)(2,1)S(1)} collective-permute-done((bf16[1,32,256]{2,1,0:T(8,128)(2,1)S(1)}, bf16[1,32,256]{2,1,0:T(8,128)(2,1)S(1)}, u32[]{:S(2)}, u32[]{:S(2)}) %collective-permute-start.13) | collective-permute-done | bytes 16416 | tf_op jit(solution)/shard_map/ppermute | solution.py:21
  106.2 7.7 %collective-permute-start.14 = (bf16[10,1,256]{2,1,0:T(2,128)(2,1)S(1)}, bf16[10,1,256]{2,1,0:T(2,128)(2,1)S(1)}, u32[]{:S(2)}, u32[]{:S(2)}) collective-permute-start(bf16[10,1,256]{2,1,0:T(2,128)(2,1)S(1)} %get-tuple-element.9), channel_id=1, source_target_pairs={{0,1},{1,2},{2,3},{3,4},{4,5},{5,6},{6,7},{7,8},{8,9},{9,10},{10,1... | collective-permute-start | bytes 15368 | tf_op jit(solution)/shard_map/ppermute | solution.py:19
  115.4 3.4 %collective-permute-done.15 = bf16[10,1,256]{2,1,0:T(2,128)(2,1)S(1)} collective-permute-done((bf16[10,1,256]{2,1,0:T(2,128)(2,1)S(1)}, bf16[10,1,256]{2,1,0:T(2,128)(2,1)S(1)}, u32[]{:S(2)}, u32[]{:S(2)}) %collective-permute-start.15) | collective-permute-done | bytes 5152 | tf_op jit(solution)/shard_map/ppermute | solution.py:21
  118.9 6.9 %gather_fusion.3 = bf16[2304,256]{1,0:T(8,128)(2,1)S(1)} fusion(bf16[341,256]{1,0:T(8,128)(2,1)S(1)} %concatenate.65, s32[3072]{0:T(1024)S(1)} %pad_clamp_fusion), kind=kCustom, calls=%fused_computation.3.clone | custom fusion | bytes 2368512 | tf_op jit(solution)/shard_map/jit(_take)/gather | solution.py:76
  131.7 2.9 collective-permute-start.16
  136.5 3.1 %collective-permute-done.17 = bf16[1,32,256]{2,1,0:T(8,128)(2,1)S(1)} collective-permute-done((bf16[1,32,256]{2,1,0:T(8,128)(2,1)S(1)}, bf16[1,32,256]{2,1,0:T(8,128)(2,1)S(1)}, u32[]{:S(2)}, u32[]{:S(2)}) %collective-permute-start.17) | collective-permute-done | bytes 16416 | tf_op jit(solution)/shard_map/ppermute | solution.py:21
  139.7 7.7 %collective-permute-start.18 = (bf16[10,1,256]{2,1,0:T(2,128)(2,1)S(1)}, bf16[10,1,256]{2,1,0:T(2,128)(2,1)S(1)}, u32[]{:S(2)}, u32[]{:S(2)}) collective-permute-start(bf16[10,1,256]{2,1,0:T(2,128)(2,1)S(1)} %get-tuple-element.7), channel_id=1, source_target_pairs={{0,1},{1,2},{2,3},{3,4},{4,5},{5,6},{6,7},{7,8},{8,9},{9,10},{10,1... | collective-permute-start | bytes 15368 | tf_op jit(solution)/shard_map/ppermute | solution.py:19
  148.7 3.5 %collective-permute-done.19 = bf16[10,1,256]{2,1,0:T(2,128)(2,1)S(1)} collective-permute-done((bf16[10,1,256]{2,1,0:T(2,128)(2,1)S(1)}, bf16[10,1,256]{2,1,0:T(2,128)(2,1)S(1)}, u32[]{:S(2)}, u32[]{:S(2)}) %collective-permute-start.19) | collective-permute-done | bytes 5152 | tf_op jit(solution)/shard_map/ppermute | solution.py:21
  152.4 6.9 %gather_fusion.4 = bf16[2304,256]{1,0:T(8,128)(2,1)S(1)} fusion(bf16[341,256]{1,0:T(8,128)(2,1)S(1)} %concatenate.68, s32[3072]{0:T(1024)S(1)} %pad_clamp_fusion), kind=kCustom, calls=%fused_computation.4.clone | custom fusion | bytes 2368512 | tf_op jit(solution)/shard_map/jit(_take)/gather | solution.py:76
  166.4 2.9 collective-permute-start.20
  171.3 3.1 %collective-permute-done.21 = bf16[1,32,256]{2,1,0:T(8,128)(2,1)S(1)} collective-permute-done((bf16[1,32,256]{2,1,0:T(8,128)(2,1)S(1)}, bf16[1,32,256]{2,1,0:T(8,128)(2,1)S(1)}, u32[]{:S(2)}, u32[]{:S(2)}) %collective-permute-start.21) | collective-permute-done | bytes 16416 | tf_op jit(solution)/shard_map/ppermute | solution.py:21
  174.4 7.6 %collective-permute-start.22 = (bf16[10,1,256]{2,1,0:T(2,128)(2,1)S(1)}, bf16[10,1,256]{2,1,0:T(2,128)(2,1)S(1)}, u32[]{:S(2)}, u32[]{:S(2)}) collective-permute-start(bf16[10,1,256]{2,1,0:T(2,128)(2,1)S(1)} %get-tuple-element.5), channel_id=1, source_target_pairs={{0,1},{1,2},{2,3},{3,4},{4,5},{5,6},{6,7},{7,8},{8,9},{9,10},{10,1... | collective-permute-start | bytes 15368 | tf_op jit(solution)/shard_map/ppermute | solution.py:19
  183.6 3.3 %collective-permute-done.23 = bf16[10,1,256]{2,1,0:T(2,128)(2,1)S(1)} collective-permute-done((bf16[10,1,256]{2,1,0:T(2,128)(2,1)S(1)}, bf16[10,1,256]{2,1,0:T(2,128)(2,1)S(1)}, u32[]{:S(2)}, u32[]{:S(2)}) %collective-permute-start.23) | collective-permute-done | bytes 5152 | tf_op jit(solution)/shard_map/ppermute | solution.py:21
  187.1 6.9 %gather_fusion.5 = bf16[2304,256]{1,0:T(8,128)(2,1)S(1)} fusion(bf16[341,256]{1,0:T(8,128)(2,1)S(1)} %concatenate.71, s32[3072]{0:T(1024)S(1)} %pad_clamp_fusion), kind=kCustom, calls=%fused_computation.5.clone | custom fusion | bytes 2368512 | tf_op jit(solution)/shard_map/jit(_take)/gather | solution.py:76
  200.9 10.9 %reshape_reshape.3 = f32[4,2,16,2,64,4]{5,4,3,2,1,0:T(8,128)} reshape(f32[8,32,256]{2,1,0:T(8,128)} %fusion) | data formatting | bytes 524288 | tf_op jit(solution)/shard_map/reshape;reshape | solution.py:31
  211.8 5.7 %reduce_sum.9 = f32[4,2,16,2,64]{4,3,2,1,0:T(2,128)S(1)} reduce(f32[4,2,16,2,64,4]{5,4,3,2,1,0:T(8,128)} %reshape_reshape.3, f32[]{:T(128)} %constant.74.clone.1), dimensions={5}, to_apply=%region_0.2 | reduce | flops 49152 | bytes 327684 | tf_op jit(solution)/shard_map/reduce_sum | solution.py:31
  218.0 76.7 %all_to_all.5 = f32[32,4,16,256]{3,2,1,0:T(8,128)S(1)} all-to-all(f32[32,4,16,256]{3,2,1,0:T(8,128)S(1)} %stack.3), channel_id=1, replica_groups=mesh['frow'=8,'fcol'=32] {'fcol'}, dimensions={0} | all-to-all | bytes 4194304 | tf_op jit(solution)/shard_map/all_to_all | solution.py:83
  (94 shorter events, 64.2 us)
Async XLA Ops:
  0.6 29.7 %copy-start = (bf16[9,256,256]{2,1,0:T(8,128)(2,1)S(1)}, bf16[9,256,256]{2,1,0:T(8,128)(2,1)}, u32[]{:S(2)}) copy-start(bf16[9,256,256]{2,1,0:T(8,128)(2,1)} %param.8) | copy-start | bytes 3538948
  1.7 7.2 %collective-permute-start = (bf16[1,32,256]{2,1,0:T(8,128)(2,1)S(1)}, bf16[1,32,256]{2,1,0:T(8,128)(2,1)S(1)}, u32[]{:S(2)}, u32[]{:S(2)}) collective-permute-start(bf16[1,32,256]{2,1,0:T(8,128)(2,1)S(1)} %get-tuple-element.27), channel_id=1, source_target_pairs={{0,32},{32,64},{64,96},{96,128},{128,160},{160,192},{192,224},{1,3... | collective-permute-start | bytes 49160 | tf_op jit(solution)/shard_map/ppermute | solution.py:19
  5.8 5.1 %collective-permute-start.1 = (bf16[1,32,256]{2,1,0:T(8,128)(2,1)S(1)}, bf16[1,32,256]{2,1,0:T(8,128)(2,1)S(1)}, u32[]{:S(2)}, u32[]{:S(2)}) collective-permute-start(bf16[1,32,256]{2,1,0:T(8,128)(2,1)S(1)} %get-tuple-element.28), channel_id=1, source_target_pairs={{32,0},{64,32},{96,64},{128,96},{160,128},{192,160},{224,192},{33,... | collective-permute-start | bytes 49160 | tf_op jit(solution)/shard_map/ppermute | solution.py:21
  10.9 4.5 %collective-permute-start.2 = (bf16[10,1,256]{2,1,0:T(2,128)(2,1)S(1)}, bf16[10,1,256]{2,1,0:T(2,128)(2,1)S(1)}, u32[]{:S(2)}, u32[]{:S(2)}) collective-permute-start(bf16[10,1,256]{2,1,0:T(2,128)(2,1)S(1)} %get-tuple-element.15), channel_id=1, source_target_pairs={{0,1},{1,2},{2,3},{3,4},{4,5},{5,6},{6,7},{7,8},{8,9},{9,10},{10,1... | collective-permute-start | bytes 15368 | tf_op jit(solution)/shard_map/ppermute | solution.py:19
  14.1 4.4 %collective-permute-start.3 = (bf16[10,1,256]{2,1,0:T(2,128)(2,1)S(1)}, bf16[10,1,256]{2,1,0:T(2,128)(2,1)S(1)}, u32[]{:S(2)}, u32[]{:S(2)}) collective-permute-start(bf16[10,1,256]{2,1,0:T(2,128)(2,1)S(1)} %get-tuple-element.16), channel_id=1, source_target_pairs={{1,0},{2,1},{3,2},{4,3},{5,4},{6,5},{7,6},{8,7},{9,8},{10,9},{11,1... | collective-permute-start | bytes 15368 | tf_op jit(solution)/shard_map/ppermute | solution.py:21
  27.6 2.7 copy-start.1
  27.6 2.7 copy-start.2
  30.9 29.7 %copy-start.3 = (f32[8,32,256]{2,1,0:T(8,128)}, f32[8,32,256]{2,1,0:T(8,128)S(1)}, u32[]{:S(2)}) copy-start(f32[8,32,256]{2,1,0:T(8,128)S(1)} %get-tuple-element.30) | copy-start | bytes 786436
  30.9 5.3 %collective-permute-start.4 = (bf16[1,32,256]{2,1,0:T(8,128)(2,1)S(1)}, bf16[1,32,256]{2,1,0:T(8,128)(2,1)S(1)}, u32[]{:S(2)}, u32[]{:S(2)}) collective-permute-start(bf16[1,32,256]{2,1,0:T(8,128)(2,1)S(1)} %get-tuple-element.25), channel_id=1, source_target_pairs={{0,32},{32,64},{64,96},{96,128},{128,160},{160,192},{192,224},{1,3... | collective-permute-start | bytes 49160 | tf_op jit(solution)/shard_map/ppermute | solution.py:19
  34.3 5.1 %collective-permute-start.5 = (bf16[1,32,256]{2,1,0:T(8,128)(2,1)S(1)}, bf16[1,32,256]{2,1,0:T(8,128)(2,1)S(1)}, u32[]{:S(2)}, u32[]{:S(2)}) collective-permute-start(bf16[1,32,256]{2,1,0:T(8,128)(2,1)S(1)} %get-tuple-element.26), channel_id=1, source_target_pairs={{32,0},{64,32},{96,64},{128,96},{160,128},{192,160},{224,192},{33,... | collective-permute-start | bytes 49160 | tf_op jit(solution)/shard_map/ppermute | solution.py:21
  39.4 4.5 %collective-permute-start.6 = (bf16[10,1,256]{2,1,0:T(2,128)(2,1)S(1)}, bf16[10,1,256]{2,1,0:T(2,128)(2,1)S(1)}, u32[]{:S(2)}, u32[]{:S(2)}) collective-permute-start(bf16[10,1,256]{2,1,0:T(2,128)(2,1)S(1)} %get-tuple-element.13), channel_id=1, source_target_pairs={{0,1},{1,2},{2,3},{3,4},{4,5},{5,6},{6,7},{7,8},{8,9},{9,10},{10,1... | collective-permute-start | bytes 15368 | tf_op jit(solution)/shard_map/ppermute | solution.py:19
  42.6 6.3 %collective-permute-start.7 = (bf16[10,1,256]{2,1,0:T(2,128)(2,1)S(1)}, bf16[10,1,256]{2,1,0:T(2,128)(2,1)S(1)}, u32[]{:S(2)}, u32[]{:S(2)}) collective-permute-start(bf16[10,1,256]{2,1,0:T(2,128)(2,1)S(1)} %get-tuple-element.14), channel_id=1, source_target_pairs={{1,0},{2,1},{3,2},{4,3},{5,4},{6,5},{7,6},{8,7},{9,8},{10,9},{11,1... | collective-permute-start | bytes 15368 | tf_op jit(solution)/shard_map/ppermute | solution.py:21
  61.8 4.9 %collective-permute-start.8 = (bf16[1,32,256]{2,1,0:T(8,128)(2,1)S(1)}, bf16[1,32,256]{2,1,0:T(8,128)(2,1)S(1)}, u32[]{:S(2)}, u32[]{:S(2)}) collective-permute-start(bf16[1,32,256]{2,1,0:T(8,128)(2,1)S(1)} %get-tuple-element.23), channel_id=1, source_target_pairs={{0,32},{32,64},{64,96},{96,128},{128,160},{160,192},{192,224},{1,3... | collective-permute-start | bytes 49160 | tf_op jit(solution)/shard_map/ppermute | solution.py:19
  64.7 5.1 %collective-permute-start.9 = (bf16[1,32,256]{2,1,0:T(8,128)(2,1)S(1)}, bf16[1,32,256]{2,1,0:T(8,128)(2,1)S(1)}, u32[]{:S(2)}, u32[]{:S(2)}) collective-permute-start(bf16[1,32,256]{2,1,0:T(8,128)(2,1)S(1)} %get-tuple-element.24), channel_id=1, source_target_pairs={{32,0},{64,32},{96,64},{128,96},{160,128},{192,160},{224,192},{33,... | collective-permute-start | bytes 49160 | tf_op jit(solution)/shard_map/ppermute | solution.py:21
  69.8 11.0 %collective-permute-start.10 = (bf16[10,1,256]{2,1,0:T(2,128)(2,1)S(1)}, bf16[10,1,256]{2,1,0:T(2,128)(2,1)S(1)}, u32[]{:S(2)}, u32[]{:S(2)}) collective-permute-start(bf16[10,1,256]{2,1,0:T(2,128)(2,1)S(1)} %get-tuple-element.11), channel_id=1, source_target_pairs={{0,1},{1,2},{2,3},{3,4},{4,5},{5,6},{6,7},{7,8},{8,9},{9,10},{10,1... | collective-permute-start | bytes 15368 | tf_op jit(solution)/shard_map/ppermute | solution.py:19
  79.5 4.9 %collective-permute-start.11 = (bf16[10,1,256]{2,1,0:T(2,128)(2,1)S(1)}, bf16[10,1,256]{2,1,0:T(2,128)(2,1)S(1)}, u32[]{:S(2)}, u32[]{:S(2)}) collective-permute-start(bf16[10,1,256]{2,1,0:T(2,128)(2,1)S(1)} %get-tuple-element.12), channel_id=1, source_target_pairs={{1,0},{2,1},{3,2},{4,3},{5,4},{6,5},{7,6},{8,7},{9,8},{10,9},{11,1... | collective-permute-start | bytes 15368 | tf_op jit(solution)/shard_map/ppermute | solution.py:21
  98.2 4.9 %collective-permute-start.12 = (bf16[1,32,256]{2,1,0:T(8,128)(2,1)S(1)}, bf16[1,32,256]{2,1,0:T(8,128)(2,1)S(1)}, u32[]{:S(2)}, u32[]{:S(2)}) collective-permute-start(bf16[1,32,256]{2,1,0:T(8,128)(2,1)S(1)} %get-tuple-element.21), channel_id=1, source_target_pairs={{0,32},{32,64},{64,96},{96,128},{128,160},{160,192},{192,224},{1,3... | collective-permute-start | bytes 49160 | tf_op jit(solution)/shard_map/ppermute | solution.py:19
  101.1 5.1 %collective-permute-start.13 = (bf16[1,32,256]{2,1,0:T(8,128)(2,1)S(1)}, bf16[1,32,256]{2,1,0:T(8,128)(2,1)S(1)}, u32[]{:S(2)}, u32[]{:S(2)}) collective-permute-start(bf16[1,32,256]{2,1,0:T(8,128)(2,1)S(1)} %get-tuple-element.22), channel_id=1, source_target_pairs={{32,0},{64,32},{96,64},{128,96},{160,128},{192,160},{224,192},{33,... | collective-permute-start | bytes 49160 | tf_op jit(solution)/shard_map/ppermute | solution.py:21
  106.2 9.1 %collective-permute-start.14 = (bf16[10,1,256]{2,1,0:T(2,128)(2,1)S(1)}, bf16[10,1,256]{2,1,0:T(2,128)(2,1)S(1)}, u32[]{:S(2)}, u32[]{:S(2)}) collective-permute-start(bf16[10,1,256]{2,1,0:T(2,128)(2,1)S(1)} %get-tuple-element.9), channel_id=1, source_target_pairs={{0,1},{1,2},{2,3},{3,4},{4,5},{5,6},{6,7},{7,8},{8,9},{9,10},{10,1... | collective-permute-start | bytes 15368 | tf_op jit(solution)/shard_map/ppermute | solution.py:19
  113.9 4.9 %collective-permute-start.15 = (bf16[10,1,256]{2,1,0:T(2,128)(2,1)S(1)}, bf16[10,1,256]{2,1,0:T(2,128)(2,1)S(1)}, u32[]{:S(2)}, u32[]{:S(2)}) collective-permute-start(bf16[10,1,256]{2,1,0:T(2,128)(2,1)S(1)} %get-tuple-element.10), channel_id=1, source_target_pairs={{1,0},{2,1},{3,2},{4,3},{5,4},{6,5},{7,6},{8,7},{9,8},{10,9},{11,1... | collective-permute-start | bytes 15368 | tf_op jit(solution)/shard_map/ppermute | solution.py:21
  131.7 4.9 %collective-permute-start.16 = (bf16[1,32,256]{2,1,0:T(8,128)(2,1)S(1)}, bf16[1,32,256]{2,1,0:T(8,128)(2,1)S(1)}, u32[]{:S(2)}, u32[]{:S(2)}) collective-permute-start(bf16[1,32,256]{2,1,0:T(8,128)(2,1)S(1)} %get-tuple-element.19), channel_id=1, source_target_pairs={{0,32},{32,64},{64,96},{96,128},{128,160},{160,192},{192,224},{1,3... | collective-permute-start | bytes 49160 | tf_op jit(solution)/shard_map/ppermute | solution.py:19
  134.6 5.1 %collective-permute-start.17 = (bf16[1,32,256]{2,1,0:T(8,128)(2,1)S(1)}, bf16[1,32,256]{2,1,0:T(8,128)(2,1)S(1)}, u32[]{:S(2)}, u32[]{:S(2)}) collective-permute-start(bf16[1,32,256]{2,1,0:T(8,128)(2,1)S(1)} %get-tuple-element.20), channel_id=1, source_target_pairs={{32,0},{64,32},{96,64},{128,96},{160,128},{192,160},{224,192},{33,... | collective-permute-start | bytes 49160 | tf_op jit(solution)/shard_map/ppermute | solution.py:21
  139.7 9.0 %collective-permute-start.18 = (bf16[10,1,256]{2,1,0:T(2,128)(2,1)S(1)}, bf16[10,1,256]{2,1,0:T(2,128)(2,1)S(1)}, u32[]{:S(2)}, u32[]{:S(2)}) collective-permute-start(bf16[10,1,256]{2,1,0:T(2,128)(2,1)S(1)} %get-tuple-element.7), channel_id=1, source_target_pairs={{0,1},{1,2},{2,3},{3,4},{4,5},{5,6},{6,7},{7,8},{8,9},{9,10},{10,1... | collective-permute-start | bytes 15368 | tf_op jit(solution)/shard_map/ppermute | solution.py:19
  147.4 4.9 %collective-permute-start.19 = (bf16[10,1,256]{2,1,0:T(2,128)(2,1)S(1)}, bf16[10,1,256]{2,1,0:T(2,128)(2,1)S(1)}, u32[]{:S(2)}, u32[]{:S(2)}) collective-permute-start(bf16[10,1,256]{2,1,0:T(2,128)(2,1)S(1)} %get-tuple-element.8), channel_id=1, source_target_pairs={{1,0},{2,1},{3,2},{4,3},{5,4},{6,5},{7,6},{8,7},{9,8},{10,9},{11,1... | collective-permute-start | bytes 15368 | tf_op jit(solution)/shard_map/ppermute | solution.py:21
  166.4 4.9 %collective-permute-start.20 = (bf16[1,32,256]{2,1,0:T(8,128)(2,1)S(1)}, bf16[1,32,256]{2,1,0:T(8,128)(2,1)S(1)}, u32[]{:S(2)}, u32[]{:S(2)}) collective-permute-start(bf16[1,32,256]{2,1,0:T(8,128)(2,1)S(1)} %get-tuple-element.17), channel_id=1, source_target_pairs={{0,32},{32,64},{64,96},{96,128},{128,160},{160,192},{192,224},{1,3... | collective-permute-start | bytes 49160 | tf_op jit(solution)/shard_map/ppermute | solution.py:19
  169.4 5.1 %collective-permute-start.21 = (bf16[1,32,256]{2,1,0:T(8,128)(2,1)S(1)}, bf16[1,32,256]{2,1,0:T(8,128)(2,1)S(1)}, u32[]{:S(2)}, u32[]{:S(2)}) collective-permute-start(bf16[1,32,256]{2,1,0:T(8,128)(2,1)S(1)} %get-tuple-element.18), channel_id=1, source_target_pairs={{32,0},{64,32},{96,64},{128,96},{160,128},{192,160},{224,192},{33,... | collective-permute-start | bytes 49160 | tf_op jit(solution)/shard_map/ppermute | solution.py:21
  174.4 9.2 %collective-permute-start.22 = (bf16[10,1,256]{2,1,0:T(2,128)(2,1)S(1)}, bf16[10,1,256]{2,1,0:T(2,128)(2,1)S(1)}, u32[]{:S(2)}, u32[]{:S(2)}) collective-permute-start(bf16[10,1,256]{2,1,0:T(2,128)(2,1)S(1)} %get-tuple-element.5), channel_id=1, source_target_pairs={{0,1},{1,2},{2,3},{3,4},{4,5},{5,6},{6,7},{7,8},{8,9},{9,10},{10,1... | collective-permute-start | bytes 15368 | tf_op jit(solution)/shard_map/ppermute | solution.py:19
  182.1 4.8 %collective-permute-start.23 = (bf16[10,1,256]{2,1,0:T(2,128)(2,1)S(1)}, bf16[10,1,256]{2,1,0:T(2,128)(2,1)S(1)}, u32[]{:S(2)}, u32[]{:S(2)}) collective-permute-start(bf16[10,1,256]{2,1,0:T(2,128)(2,1)S(1)} %get-tuple-element.6), channel_id=1, source_target_pairs={{1,0},{2,1},{3,2},{4,3},{5,4},{6,5},{7,6},{8,7},{9,8},{10,9},{11,1... | collective-permute-start | bytes 15368 | tf_op jit(solution)/shard_map/ppermute | solution.py:21
  196.0 2.7 copy-start.4
